TPU v7x, 128 devices: a whole 4x4x4 slice. The times are simulated.
128 devices in a mesh: grp: 8 (over y, core), seq: 16 (over z, x).
Axes of the slice: x: 4, y: 4, z: 4, core: 2. Of those that a mesh axis runs over, the one named last changes fastest.
Arguments:
- queries: bfloat16 [131072, 1024], P(('grp', 'seq')), may hold values from -6 to 6
- key_rows: bfloat16 [131072, 1024], P(('grp', 'seq')), may hold values from -6 to 6
- value_rows: bfloat16 [131072, 1024], P(('grp', 'seq')), may hold values from -6 to 6
- norm_gain: float32 [1024], replicated, may hold values from 0.25 to 1.75
- cotangent: bfloat16 [131072, 1024], P(('grp', 'seq')), may hold values from -6 to 6
Outputs:
- normed_out: bfloat16 [131072, 1024], P(('grp', 'seq'))
- grad_queries: bfloat16 [131072, 1024], P(('grp', 'seq'))
- grad_keys: bfloat16 [131072, 1024], P(('grp', 'seq'))
- grad_values: bfloat16 [131072, 1024], P(('grp', 'seq'))
All inputs are finite; a program needn't handle non-finite values.
Results may differ from a plain program's by a relative error of at most 0.0058.
Values sent between devices are 32-bit elements; how exact they have to be, the bound alone decides.
A program may use at most 128 MiB of HBM per device.

v0:
```python
import jax
import jax.numpy as jnp
from jax import lax
from jax.sharding import PartitionSpec as P

H = 8
HD = 128
BLOCK = 512


EPSILON = 1e-06


def carried_in(part, axis, combine, identity, reverse):
    count = lax.axis_size(axis)
    place = lax.axis_index(axis)
    ahead = count - 1 - place if reverse else place
    gathered = lax.all_gather(part, axis)
    state = jnp.zeros_like(part) + jnp.asarray(identity, part.dtype)

    def one(step, state):
        source = count - 1 - step if reverse else step
        return combine(state, lax.dynamic_index_in_dim(gathered, source, 0, False))

    return lax.fori_loop(0, ahead, one, state)


def lower_mask(length):
    indices = jnp.arange(length)
    return indices[:, None] >= indices[None, :]


def add_states(earlier, later):
    return earlier + later


def carried(own_total, reverse):
    zero_state = jnp.zeros_like(own_total)
    within = carried_in(own_total, "seq", add_states, zero_state, reverse)
    group_sum = lax.psum(own_total, "seq")
    before = carried_in(group_sum, "grp", add_states, zero_state, reverse)
    return within + before


def body(queries, key_rows, value_rows, norm_gain, cotangent):
    tokens, features = queries.shape
    block_count = tokens // BLOCK
    block_shape = (block_count, BLOCK, H, HD)
    query_blocks = queries.reshape(block_shape)
    key_blocks = key_rows.reshape(block_shape)
    value_blocks = value_rows.reshape(block_shape)
    causal = lower_mask(BLOCK)[None, None]
    block_states = jnp.einsum(
        "bshd,bshe->bhde", key_blocks, value_blocks, preferred_element_type=jnp.float32
    )
    own_total = jnp.sum(block_states, axis=0)
    inside = jnp.cumsum(block_states, axis=0) - block_states
    scores = jnp.einsum(
        "bthd,bshd->bhts", query_blocks, key_blocks, preferred_element_type=jnp.float32
    )
    scores = jnp.where(causal, scores, 0.0).astype(jnp.bfloat16)
    local_part = jnp.einsum(
        "bhts,bshe->bthe", scores, value_blocks, preferred_element_type=jnp.float32
    )
    prior_state = (carried(own_total, False) + inside).astype(jnp.bfloat16)
    attended = local_part + jnp.einsum(
        "bthd,bhde->bthe", query_blocks, prior_state, preferred_element_type=jnp.float32
    )
    attended = attended.reshape(tokens, features)
    inverse = lax.rsqrt(jnp.mean(attended * attended, axis=1, keepdims=True) + EPSILON)
    unit_rows = attended * inverse
    gain_rows = norm_gain[None, :]
    normed_out = (unit_rows * gain_rows).astype(jnp.bfloat16)
    scaled = cotangent.astype(jnp.float32) * gain_rows
    grad_attended = inverse * (
        scaled - unit_rows * jnp.mean(scaled * unit_rows, axis=1, keepdims=True)
    )
    grad_blocks = grad_attended.astype(jnp.bfloat16).reshape(block_shape)
    grad_states = jnp.einsum(
        "bthd,bthe->bhde", query_blocks, grad_blocks, preferred_element_type=jnp.float32
    )
    grad_total = jnp.sum(grad_states, axis=0)
    later_inside = jnp.cumsum(grad_states[::-1], axis=0)[::-1] - grad_states
    grad_scores = jnp.einsum(
        "bthe,bshe->bhts", grad_blocks, value_blocks, preferred_element_type=jnp.float32
    )
    grad_scores = jnp.where(causal, grad_scores, 0.0).astype(jnp.bfloat16)
    local_q = jnp.einsum(
        "bhts,bshd->bthd", grad_scores, key_blocks, preferred_element_type=jnp.float32
    )
    local_k = jnp.einsum(
        "bhts,bthd->bshd", grad_scores, query_blocks, preferred_element_type=jnp.float32
    )
    local_v = jnp.einsum("bhts,bthe->bshe", scores, grad_blocks, preferred_element_type=jnp.float32)
    later_state = (carried(grad_total, True) + later_inside).astype(jnp.bfloat16)
    grad_q = local_q + jnp.einsum(
        "bthe,bhde->bthd", grad_blocks, prior_state, preferred_element_type=jnp.float32
    )
    grad_k = local_k + jnp.einsum(
        "bshe,bhde->bshd", value_blocks, later_state, preferred_element_type=jnp.float32
    )
    grad_v = local_v + jnp.einsum(
        "bshd,bhde->bshe", key_blocks, later_state, preferred_element_type=jnp.float32
    )
    return (
        normed_out,
        grad_q.astype(jnp.bfloat16).reshape(tokens, features),
        grad_k.astype(jnp.bfloat16).reshape(tokens, features),
        grad_v.astype(jnp.bfloat16).reshape(tokens, features),
    )


def solution(mesh):
    return jax.shard_map(
        body,
        mesh=mesh,
        in_specs=(
            P(("grp", "seq"), None),
            P(("grp", "seq"), None),
            P(("grp", "seq"), None),
            P(),
            P(("grp", "seq"), None),
        ),
        out_specs=(
            P(("grp", "seq"), None),
            P(("grp", "seq"), None),
            P(("grp", "seq"), None),
            P(("grp", "seq"), None),
        ),
        check_vma=False,
    )
```

profile of v0, /device:TPU:1, one launch (start us, length us, event | category | flops | bytes accessed | tf_op | source)
XLA Modules:
  0.0 489.7 jit_solution(6955377687999199124)
XLA Ops:
  11.0 2.9 fusion.22
  13.9 74.2 %all-gather.11.cloned.1.call-done = f32[128,128,128]{2,1,0:T(8,128)} async-done(((f32[8,128,128]{2,1,0:T(8,128)}), f32[128,128,128]{2,1,0:T(8,128)}) %all-gather.11.cloned.1.call-update) | async-done | bytes 8388624 | tf_op jit(solution)/shard_map/all_gather | solution.py:18
  88.9 87.4 %all-reduce.3.cloned.1.call-done = f32[1,8,128,128]{3,2,1,0:T(8,128)} async-done(((f32[1,8,128,128]{3,2,1,0:T(8,128)}), f32[1,8,128,128]{3,2,1,0:T(8,128)}) %all-reduce.3.cloned.1.call-update) | async-done | bytes 524304 | tf_op jit(solution)/shard_map/psum | solution.py:40
  178.9 2.5 select_convert_fusion.1
  181.3 8.0 %fusion.6 = f32[2,8,512,128]{2,3,1,0:T(8,128)} fusion(bf16[2,8,512,512]{3,2,1,0:T(8,128)(2,1)S(1)} %select_convert_fusion.1, bf16[2,512,8,128]{3,2,1,0:T(8,128)(2,1)} %bitcast.104), kind=kOutput, calls=%fused_computation.27 | convolution fusion | flops 1073741824 | bytes 14680064 | tf_op jit(solution)/shard_map/bhts,bshe->bthe/dot_general | solution.py:62
  189.4 21.9 %all-gather.7.cloned.1.call-done = f32[8,8,128,128]{3,2,1,0:T(8,128)} async-done(((f32[1,8,128,128]{3,2,1,0:T(8,128)}), f32[8,8,128,128]{3,2,1,0:T(8,128)}) %all-gather.7.cloned.1.call-update) | async-done | bytes 4194320 | tf_op jit(solution)/shard_map/all_gather | solution.py:18
  215.6 3.0 multiply_reduce_fusion.1
  218.6 5.5 %copy.64 = f32[2,512,8,128]{3,2,1,0:T(8,128)} copy(f32[2,512,8,128]{1,3,2,0:T(8,128)} %get-tuple-element.203) | data formatting | bytes 8388608 | tf_op jit(solution)/shard_map/add | solution.py:66
  224.1 3.5 multiply_reduce_fusion
  227.7 2.6 fusion.2
  232.2 3.0 copy.73
  235.2 3.2 fusion.23
  241.1 93.8 %all-reduce.5.cloned.1.call-done = f32[1,8,128,128]{2,3,1,0:T(8,128)} async-done(((f32[1,8,128,128]{2,3,1,0:T(8,128)}), f32[1,8,128,128]{2,3,1,0:T(8,128)}) %all-reduce.5.cloned.1.call-update) | async-done | bytes 524304 | tf_op jit(solution)/shard_map/psum | solution.py:40
  338.6 4.3 select_convert_fusion
  351.5 3.2 fusion.25
  354.7 4.5 fusion.18
  359.2 11.1 %all-gather.9.cloned.1.call-done = f32[8,8,128,128]{3,2,1,0:T(8,128)} async-done(((f32[1,8,128,128]{3,2,1,0:T(8,128)}), f32[8,8,128,128]{3,2,1,0:T(8,128)}) %all-gather.9.cloned.1.call-update) | async-done | bytes 4194320 | tf_op jit(solution)/shard_map/all_gather | solution.py:18
  370.3 7.2 %while.47 = (s32[]{:T(128)}, f32[8,128,128]{2,1,0:T(8,128)S(1)}, s32[]{:T(128)}, f32[8,8,128,128]{3,2,1,0:T(8,128)}, s32[]{:T(128)}, /*index=5*/s32[]{:T(128)}, s32[]{:T(128)}, s32[]{:T(128)}) while((s32[]{:T(128)}, f32[8,128,128]{2,1,0:T(8,128)S(1)}, s32[]{:T(128)}, f32[8,8,128,128]{3,2,1,0:T(8,128)}, s32[]{:T(128)}, ...), condition=%wide.region_14.15_spmd, body=%wide.region_13.14_spmd.sunk | while | flops 131078 | bytes 1573007 | solution.py:25
  377.5 65.2 %all-gather.13.cloned.1.call-done = f32[128,128,128]{2,1,0:T(8,128)} async-done(((f32[8,128,128]{2,1,0:T(8,128)}), f32[128,128,128]{2,1,0:T(8,128)}) %all-gather.13.cloned.1.call-update) | async-done | bytes 8388624 | tf_op jit(solution)/shard_map/all_gather | solution.py:18
  442.7 18.1 %while.46 = (s32[]{:T(128)}, f32[8,128,128]{2,1,0:T(8,128)S(1)}, s32[]{:T(128)}, f32[16,8,128,128]{3,2,1,0:T(8,128)}, s32[]{:T(128)}, /*index=5*/s32[]{:T(128)}, s32[]{:T(128)}, s32[]{:T(128)}) while((s32[]{:T(128)}, f32[8,128,128]{2,1,0:T(8,128)S(1)}, s32[]{:T(128)}, f32[16,8,128,128]{3,2,1,0:T(8,128)}, s32[]{:T(128)}, ...), condition=%wide.region_11.12_spmd, body=%wide.region_10.11_spmd.sunk | while | flops 131078 | bytes 1573007 | solution.py:25
  466.2 4.4 fusion.3
  470.6 4.4 copy.84
  475.1 2.9 fusion
  479.5 3.3 copy_bitcast_fusion
  (107 shorter events, 60.7 us)
Async XLA Ops:
  7.2 81.0 %all-gather.11.cloned.1.call-start = ((), (), s32[]{:S(2)}) async-start(), calls=%async_computation.4 | async-start | bytes 8912896 | tf_op jit(solution)/shard_map/all_gather | solution.py:18
  7.2 2.4 copy-start.18
  10.2 3.7 copy-start.4
  88.1 88.2 %all-reduce.3.cloned.1.call-start = ((), (), s32[]{:S(2)}) async-start(), calls=%async_computation | async-start | bytes 1048576 | tf_op jit(solution)/shard_map/psum | solution.py:40
  88.9 122.5 %all-gather.7.cloned.1.call-start = ((), (), s32[]{:S(2)}) async-start(), calls=%async_computation.1 | async-start | bytes 4718592 | tf_op jit(solution)/shard_map/all_gather | solution.py:18
  176.4 2.5 copy-start.7
  178.8 36.0 %copy-start.2 = (bf16[128,8,8,128]{3,2,1,0:T(8,128)(2,1)}, bf16[128,8,8,128]{3,2,1,0:T(8,128)(2,1)S(1)}, u32[]{:S(2)}) copy-start(bf16[128,8,8,128]{3,2,1,0:T(8,128)(2,1)S(1)} %copy.90) | copy-start | bytes 6291460
  181.3 8.1 %copy-start = (bf16[2,8,512,512]{3,2,1,0:T(8,128)(2,1)}, bf16[2,8,512,512]{3,2,1,0:T(8,128)(2,1)S(1)}, u32[]{:S(2)}) copy-start(bf16[2,8,512,512]{3,2,1,0:T(8,128)(2,1)S(1)} %select_convert_fusion.1) | copy-start | bytes 25165828
  212.8 2.8 copy-start.10
  215.6 3.0 copy-start.13
  218.6 5.5 %copy-start.11 = (bf16[1024,1024]{1,0:T(8,128)(2,1)S(1)}, bf16[1024,1024]{1,0:T(8,128)(2,1)}, u32[]{:S(2)}) copy-start(bf16[1024,1024]{1,0:T(8,128)(2,1)} %param.17) | copy-start | bytes 6291460
  218.6 5.5 %copy-start.19 = (f32[1024]{0:T(1024)S(1)}, f32[1024]{0:T(1024)}, u32[]{:S(2)}) copy-start(f32[1024]{0:T(1024)} %param.16) | copy-start | bytes 12292
  224.1 3.6 copy-start.1
  240.5 94.4 %all-reduce.5.cloned.1.call-start = ((), (), s32[]{:S(2)}) async-start(), calls=%async_computation.2 | async-start | bytes 1048576 | tf_op jit(solution)/shard_map/psum | solution.py:40
  241.0 129.2 %all-gather.9.cloned.1.call-start = ((), (), s32[]{:S(2)}) async-start(), calls=%async_computation.3 | async-start | bytes 4718592 | tf_op jit(solution)/shard_map/all_gather | solution.py:18
  337.0 105.7 %all-gather.13.cloned.1.call-start = ((), (), s32[]{:S(2)}) async-start(), calls=%async_computation.5 | async-start | bytes 8912896 | tf_op jit(solution)/shard_map/all_gather | solution.py:18
  338.6 4.3 copy-start.8
  345.3 6.1 %slice-start = ((s8[8388608]{0:T(1024)(128)(4,1)}), s8[4194304]{0:T(1024)(128)(4,1)S(1)}, s32[]{:S(2)}) async-start(s8[8388608]{0:T(1024)(128)(4,1)} %bitcast.95), calls=%async_computation.6 | async-start | bytes 8388608
  346.3 5.1 %slice-start.1 = ((s8[8388608]{0:T(1024)(128)(4,1)}), s8[4194304]{0:T(1024)(128)(4,1)S(1)}, s32[]{:S(2)}) async-start(s8[8388608]{0:T(1024)(128)(4,1)} %bitcast.95), calls=%async_computation.7 | async-start | bytes 8388608
  347.7 2.7 copy-start.17
  351.5 3.3 copy-start.3
  461.7 4.5 copy-start.9
  470.6 4.5 copy-start.5
  470.6 4.5 copy-start.16
  (4 other events, 6.1 us)
Sparse Core Ops, SparseCore 0:
  14.0 74.0 all-gather.10
  92.8 83.5 all-reduce.2
  178.2 33.1 all-gather.6
  245.1 89.7 all-reduce.4
  337.1 33.1 all-gather.8
  372.2 70.3 all-gather.12
where the time goes:
time: 491 us; the launch traced here: 490 us
  waiting for transfers between devices  355 us (72%)
  matrix products  42.2 us (9%)
  local copies, waits for them, and re-layouts  39 us (8%)
  other arithmetic  37.4 us (8%)
  between operations  14.4 us (3%)
    psum x2, waiting for transfers between devices, carried(): group_sum = lax.psum(own_total, 'seq')  181 us
    all_gather x4, waiting for transfers between devices, carried_in(): gathered = lax.all_gather(part, axis)  172 us
    add x22, other arithmetic, add_states(): return earlier + later  25.7 us
    unnamed x50, local copies, waits for them, and re-layouts  12.6 us
  transfers between devices with their start and end apart: 6, of which 6 were waited for; matrix products, arithmetic and copies ran while one was open for 8% of the time, Pallas kernels for 0%

commit v1 on v0

v1 whole, which is shorter than its diff:
```python
import functools

import jax
import jax.numpy as jnp
from jax import lax
from jax.experimental import pallas as pl
from jax.experimental.pallas import tpu as pltpu
from jax.sharding import PartitionSpec as P

H = 8
HD = 128
BLOCK = 512
HALF = 256
D = H * HD
TOK = 1024
CHUNKS = 2
HPC = H // CHUNKS
EPSILON = 1e-06
F32 = jnp.float32
BF16 = jnp.bfloat16
MESH = pl.DeviceIdType.MESH


def dot_nn(a, b):
    return lax.dot_general(a, b, (((1,), (0,)), ((), ())), preferred_element_type=F32)


def dot_nt(a, b):
    return lax.dot_general(a, b, (((1,), (1,)), ((), ())), preferred_element_type=F32)


def dot_tn(a, b):
    return lax.dot_general(a, b, (((0,), (0,)), ((), ())), preferred_element_type=F32)


def causal(tile):
    rows = lax.broadcasted_iota(jnp.int32, tile.shape, 0)
    cols = lax.broadcasted_iota(jnp.int32, tile.shape, 1)
    return jnp.where(rows >= cols, tile, 0.0)


def kernel(
    groups, shards,
    q_hbm, k_hbm, v_hbm, gain_ref, dy_hbm,
    no_hbm, gq_hbm, gk_hbm, gv_hbm,
    qh, kh, vh, dyh, sc, att, ga, lk, lv, no_s, gq_s, gk_s, gv_s,
    own, arrived, before, total, peers, result, inner, prior,
    squares, dots, inv_rows, mix_rows,
    in_sem, out_sem, send_sem, recv_sem,
):
    grp = lax.axis_index("grp")
    seq = lax.axis_index("seq")
    sub = HPC * HD // shards
    per_head = HD // sub

    def columns(h):
        return pl.ds(pl.multiple_of(h * HD, HD), HD)

    def load(i, h):
        src = (k_hbm, v_hbm, q_hbm, dy_hbm)[i]
        dst = (kh, vh, qh, dyh)[i]
        return pltpu.make_async_copy(src.at[:, columns(h)], dst.at[h], in_sem.at[i, h])

    def store(i, h):
        src = (no_s, gq_s, gk_s, gv_s)[i]
        dst = (no_hbm, gq_hbm, gk_hbm, gv_hbm)[i]
        return pltpu.make_async_copy(src.at[h], dst.at[:, columns(h)], out_sem.at[i, h])

    def each(lo, hi, fn):
        def step(h, carry):
            fn(h)
            return carry
        lax.fori_loop(lo, hi, step, 0)

    def start_loads(arrays):
        def one(h):
            for i in arrays:
                load(i, h).start()
        each(0, H, one)

    def send_parts(w, c):
        def one(d):
            to = lax.rem(seq + d, shards)
            pltpu.make_async_remote_copy(
                own.at[w, c, to], arrived.at[w, c, seq],
                send_sem.at[w, c, 0], recv_sem.at[w, c, 0],
                device_id=(grp, to), device_id_type=MESH,
            ).start()
        each(1, shards, one)
        arrived[w, c, seq] = own[w, c, seq]

    def wait_parts(w, c):
        pltpu.make_async_remote_copy(
            own.at[w, c, pl.ds(0, shards - 1)], arrived.at[w, c, pl.ds(0, shards - 1)],
            send_sem.at[w, c, 0], recv_sem.at[w, c, 0],
            device_id=(grp, seq), device_id_type=MESH,
        ).wait_recv()

    def scan_parts(w, c):
        wait_parts(w, c)
        order = range(shards) if w == 0 else range(shards - 1, -1, -1)
        running = jnp.zeros((sub, HD), F32)
        for t in order:
            before[w, c, t] = running
            running = running + arrived[w, c, t]
        total[w, c] = running

        def one(d):
            to = lax.rem(grp + d, groups)
            pltpu.make_async_remote_copy(
                total.at[w, c], peers.at[w, c, grp],
                send_sem.at[w, c, 1], recv_sem.at[w, c, 1],
                device_id=(to, seq), device_id_type=MESH,
            ).start()
        each(1, groups, one)

    def return_parts(w, c):
        pltpu.make_async_remote_copy(
            peers.at[w, c, pl.ds(0, groups - 1)], peers.at[w, c, pl.ds(0, groups - 1)],
            send_sem.at[w, c, 1], recv_sem.at[w, c, 1],
            device_id=(grp, seq), device_id_type=MESH,
        ).wait_recv()
        lo, hi = (0, grp) if w == 0 else (grp + 1, groups)
        base = lax.fori_loop(
            lo, hi, lambda g, s: s + peers[w, c, g], jnp.zeros((sub, HD), F32)
        )
        for t in range(shards):
            before[w, c, t] = before[w, c, t] + base

        def one(d):
            to = lax.rem(seq + d, shards)
            pltpu.make_async_remote_copy(
                before.at[w, c, to], result.at[w, c, seq],
                send_sem.at[w, c, 2], recv_sem.at[w, c, 2],
                device_id=(grp, to), device_id_type=MESH,
            ).start()
        each(1, shards, one)
        result[w, c, seq] = before[w, c, seq]

    def wait_result(w, c):
        pltpu.make_async_remote_copy(
            before.at[w, c, pl.ds(0, shards - 1)], result.at[w, c, pl.ds(0, shards - 1)],
            send_sem.at[w, c, 2], recv_sem.at[w, c, 2],
            device_id=(grp, seq), device_id_type=MESH,
        ).wait_recv()

    def wait_sends(w, c):
        for phase, ref, count in ((0, own, shards), (1, peers, groups), (2, before, shards)):
            pltpu.make_async_remote_copy(
                ref.at[w, c, pl.ds(0, count - 1)], ref.at[w, c, pl.ds(0, count - 1)],
                send_sem.at[w, c, phase], recv_sem.at[w, c, phase],
                device_id=(grp, seq), device_id_type=MESH,
            ).wait_send()

    def put_own(w, h, value):
        c = h // HPC
        at = pl.multiple_of((h % HPC) * per_head, per_head)
        own[w, c, pl.ds(at, per_head)] = value.reshape(per_head, sub, HD)

    def get_result(w, h):
        c = h // HPC
        at = pl.multiple_of((h % HPC) * per_head, per_head)
        return result[w, c, pl.ds(at, per_head)].reshape(HD, HD)

    def first(b, i):
        return pl.ds(b * BLOCK + i * HALF, HALF)

    def block(b):
        return pl.ds(b * BLOCK, BLOCK)

    def key_state(h):
        load(0, h).wait()
        load(1, h).wait()
        s0 = dot_tn(kh[h, block(0)], vh[h, block(0)])
        s1 = dot_tn(kh[h, block(1)], vh[h, block(1)])
        inner[0, h] = s0
        put_own(0, h, s0 + s1)

    def local(h):
        for b in range(2):
            q0, q1 = qh[h, first(b, 0)], qh[h, first(b, 1)]
            k0, k1 = kh[h, first(b, 0)], kh[h, first(b, 1)]
            v0, v1 = vh[h, first(b, 0)], vh[h, first(b, 1)]
            t00 = causal(dot_nt(q0, k0)).astype(BF16)
            t10 = dot_nt(q1, k0).astype(BF16)
            t11 = causal(dot_nt(q1, k1)).astype(BF16)
            sc[h, b, 0] = t00
            sc[h, b, 1] = t10
            sc[h, b, 2] = t11
            att[h, first(b, 0)] = dot_nn(t00, v0)
            att[h, first(b, 1)] = dot_nn(t10, v0) + dot_nn(t11, v1)

    def attend(h):
        base = get_result(0, h)
        states = (base.astype(BF16), (base + inner[0, h]).astype(BF16))
        gain = gain_ref[h]
        for b in range(2):
            prior[h, b] = states[b]
            for i in range(2):
                rows = first(b, i)
                value = att[h, rows] + dot_nn(qh[h, rows], states[b])
                att[h, rows] = value
                scaled = dyh[h, rows].astype(F32) * gain
                squares[rows] = squares[rows] + value * value
                dots[rows] = dots[rows] + scaled * value

    def row_factors():
        for b in range(2):
            for i in range(2):
                rows = first(b, i)
                mean_sq = jnp.sum(squares[rows], axis=1, keepdims=True) * (1.0 / D)
                mean_dot = jnp.sum(dots[rows], axis=1, keepdims=True) * (1.0 / D)
                inverse = lax.rsqrt(mean_sq + EPSILON)
                mix = inverse * inverse * (inverse * mean_dot)
                inv_rows[rows] = jnp.broadcast_to(inverse, (HALF, HD))
                mix_rows[rows] = jnp.broadcast_to(mix, (HALF, HD))

    def grad_state(h):
        gain = gain_ref[h]
        parts = []
        for b in range(2):
            rows = block(b)
            scaled = dyh[h, rows].astype(F32) * gain
            grad = (inv_rows[rows] * scaled - mix_rows[rows] * att[h, rows]).astype(BF16)
            ga[h, rows] = grad
            parts.append(dot_tn(qh[h, rows], grad))
        inner[1, h] = parts[1]
        put_own(1, h, parts[0] + parts[1])

    def normed(h):
        gain = gain_ref[h]
        no_s[h] = (att[h] * inv_rows[...] * gain).astype(BF16)
        store(0, h).start()

    def backward(h):
        normed(h)
        for b in range(2):
            q0, q1 = qh[h, first(b, 0)], qh[h, first(b, 1)]
            k0, k1 = kh[h, first(b, 0)], kh[h, first(b, 1)]
            v0, v1 = vh[h, first(b, 0)], vh[h, first(b, 1)]
            g0, g1 = ga[h, first(b, 0)], ga[h, first(b, 1)]
            p = prior[h, b]
            s00 = causal(dot_nt(g0, v0)).astype(BF16)
            s10 = dot_nt(g1, v0).astype(BF16)
            s11 = causal(dot_nt(g1, v1)).astype(BF16)
            gq_s[h, first(b, 0)] = (dot_nt(g0, p) + dot_nn(s00, k0)).astype(BF16)
            gq_s[h, first(b, 1)] = (dot_nt(g1, p) + dot_nn(s10, k0) + dot_nn(s11, k1)).astype(BF16)
            lk[h, first(b, 0)] = dot_tn(s00, q0) + dot_tn(s10, q1)
            lk[h, first(b, 1)] = dot_tn(s11, q1)
            lv[h, first(b, 0)] = dot_tn(sc[h, b, 0], g0) + dot_tn(sc[h, b, 1], g1)
            lv[h, first(b, 1)] = dot_tn(sc[h, b, 2], g1)
        store(1, h).start()

    def finish(h):
        base = get_result(1, h)
        states = ((base + inner[1, h]).astype(BF16), base.astype(BF16))
        for b in range(2):
            rows = block(b)
            gk_s[h, rows] = (lk[h, rows] + dot_nt(vh[h, rows], states[b])).astype(BF16)
            gv_s[h, rows] = (lv[h, rows] + dot_nn(kh[h, rows], states[b])).astype(BF16)
        store(2, h).start()
        store(3, h).start()

    start_loads((0, 1))
    barrier = pltpu.get_barrier_semaphore()

    def greet_seq(d):
        pl.semaphore_signal(
            barrier, inc=1, device_id=(grp, lax.rem(seq + d, shards)), device_id_type=MESH
        )

    def greet_grp(d):
        pl.semaphore_signal(
            barrier, inc=1, device_id=(lax.rem(grp + d, groups), seq), device_id_type=MESH
        )

    each(1, shards, greet_seq)
    each(1, groups, greet_grp)
    start_loads((2, 3))

    each(0, HPC, key_state)
    pl.semaphore_wait(barrier, shards - 1 + groups - 1)
    send_parts(0, 0)
    each(HPC, H, key_state)
    send_parts(0, 1)

    def wait_q(h):
        load(2, h).wait()
        load(3, h).wait()

    each(0, H, wait_q)
    squares[...] = jnp.zeros_like(squares)
    dots[...] = jnp.zeros_like(dots)
    each(0, 4, local)
    scan_parts(0, 0)
    each(4, 6, local)
    scan_parts(0, 1)
    return_parts(0, 0)
    each(6, 8, local)
    return_parts(0, 1)
    wait_result(0, 0)
    each(0, HPC, attend)
    wait_result(0, 1)
    each(HPC, H, attend)
    row_factors()
    each(0, HPC, grad_state)
    send_parts(1, 0)
    each(HPC, H, grad_state)
    send_parts(1, 1)
    each(0, 3, backward)
    scan_parts(1, 0)
    each(3, 5, backward)
    scan_parts(1, 1)
    return_parts(1, 0)
    each(5, 8, backward)
    return_parts(1, 1)
    wait_result(1, 0)
    each(0, HPC, finish)
    wait_result(1, 1)
    each(HPC, H, finish)
    for w in range(2):
        for c in range(CHUNKS):
            wait_sends(w, c)

    def wait_stores(h):
        for i in range(4):
            store(i, h).wait()

    each(0, H, wait_stores)


def body(groups, shards, queries, key_rows, value_rows, norm_gain, cotangent):
    sub = HPC * HD // shards
    whole = jax.ShapeDtypeStruct((TOK, D), BF16)
    anywhere = pl.BlockSpec(memory_space=pl.ANY)
    heads = lambda kind: pltpu.VMEM((H, TOK, HD), kind)
    parts = pltpu.VMEM((2, CHUNKS, shards, sub, HD), F32)
    return tuple(pl.pallas_call(
        functools.partial(kernel, groups, shards),
        out_shape=(whole,) * 4,
        in_specs=[anywhere, anywhere, anywhere, pl.BlockSpec(memory_space=pltpu.VMEM), anywhere],
        out_specs=(anywhere,) * 4,
        scratch_shapes=[
            heads(BF16), heads(BF16), heads(BF16), heads(BF16),
            pltpu.VMEM((H, 2, 3, HALF, HALF), BF16),
            heads(F32), heads(BF16), heads(F32), heads(F32),
            heads(BF16), heads(BF16), heads(BF16), heads(BF16),
            parts, parts, parts,
            pltpu.VMEM((2, CHUNKS, sub, HD), F32),
            pltpu.VMEM((2, CHUNKS, groups, sub, HD), F32),
            parts,
            pltpu.VMEM((2, H, HD, HD), F32),
            pltpu.VMEM((H, 2, HD, HD), BF16),
            pltpu.VMEM((TOK, HD), F32), pltpu.VMEM((TOK, HD), F32),
            pltpu.VMEM((TOK, HD), F32), pltpu.VMEM((TOK, HD), F32),
            pltpu.SemaphoreType.DMA((4, H)),
            pltpu.SemaphoreType.DMA((4, H)),
            pltpu.SemaphoreType.DMA((2, CHUNKS, 3)),
            pltpu.SemaphoreType.DMA((2, CHUNKS, 3)),
        ],
        compiler_params=pltpu.CompilerParams(
            collective_id=0, has_side_effects=True, vmem_limit_bytes=60 * 1024 * 1024
        ),
        name="attention",
    )(queries, key_rows, value_rows, norm_gain.reshape(H, 1, HD), cotangent))


def solution(mesh):
    rows = P(("grp", "seq"), None)
    return jax.shard_map(
        functools.partial(body, mesh.shape["grp"], mesh.shape["seq"]),
        mesh=mesh,
        in_specs=(rows, rows, rows, P(), rows),
        out_specs=(rows,) * 4,
        check_vma=False,
    )
```

time: 491 us -> 64.7 us (0.13)
  waiting for transfers between devices: 355 us -> 0 us
  Pallas kernels: 0 us -> 54.6 us
  matrix products: 42.2 us -> 0 us
  other arithmetic: 37.4 us -> 0 us
  local copies, waits for them, and re-layouts: 39 us -> 9.25 us
  between operations: 14.4 us -> 0.65 us
    psum x2 -> x0, waiting for transfers between devices: 181 us -> none  [carried(): group_sum = lax.psum(own_total, 'seq')]
    all_gather x4 -> x0, waiting for transfers between devices: 172 us -> none  [carried_in(): gathered = lax.all_gather(part, axis)]
    pallas_call x0 -> x1, Pallas kernels: none -> 54.6 us  [body(): pl.pallas_call(functools.partial(kernel, groups, shards), out_shape=(whol...]
    dot_general x12 -> x0, matrix products: 42.2 us -> none  [the longest x1 8.04 us: body(): jnp.einsum('bhts,bshe->bthe', scores, value_blocks, preferred_element_typ...]
    add x24 -> x0, other arithmetic: 26.6 us -> none  [the longest x22 25.7 us: add_states(): return earlier + later]
    add x2 -> x0, local copies, waits for them, and re-layouts: 7.7 us -> none  [the longest x1 5.5 us: body(): local_part + jnp.einsum('bthd,bhde->bthe', query_blocks, prior_state, pre...]
    convert_element_type x3 -> x0, local copies, waits for them, and re-layouts: 7.16 us -> none  [the longest x1 4.45 us: body(): grad_v.astype(jnp.bfloat16).reshape(tokens, features)]
    reshape x2 -> x0, local copies, waits for them, and re-layouts: 6.31 us -> none  [the longest x1 3.32 us: body(): grad_v.astype(jnp.bfloat16).reshape(tokens, features)]
  transfers between devices with their start and end apart: 6 -> 0, of which waited for: 6 -> 0; matrix products, arithmetic and copies ran while one was open for 8% -> 0% of each run, Pallas kernels for 0% -> 0%
where the time goes in v1:
time: 64.7 us; the launch traced here: 64.5 us
  Pallas kernels  54.6 us (84%)
  local copies, waits for them, and re-layouts  9.25 us (14%)
  between operations  0.65 us (1%)
    pallas_call x1, Pallas kernels, body(): pl.pallas_call(functools.partial(kernel, groups, shards), out_shape=(whol...  54.6 us
    unnamed x10, local copies, waits for them, and re-layouts  9.25 us

profile of v1, /device:TPU:1, one launch (start us, length us, event | category | flops | bytes accessed | tf_op | source)
XLA Modules:
  0.0 64.5 jit_solution(15160511309099417682)
XLA Ops:
  0.6 54.6 %attention.1 = (bf16[1024,1024]{1,0:T(8,128)(2,1)}, bf16[1024,1024]{1,0:T(8,128)(2,1)}, bf16[1024,1024]{1,0:T(8,128)(2,1)}, bf16[1024,1024]{1,0:T(8,128)(2,1)}) custom-call(bf16[1024,1024]{1,0:T(8,128)(2,1)} %q_hbm.1, bf16[1024,1024]{1,0:T(8,128)(2,1)} %k_hbm.1, bf16[1024,1024]{1,0:T(8,128)(2,1)} %v_hbm.1, f32[8,1,128]{2,1,0:T(1,128)} %bitcast.1, ...), custom_call_target="tpu_custom_call" | custom-call | tf_op jit(solution)/shard_map/attention/pallas_call | solution.py:338
  55.3 0.0 copy-start.2
  55.3 3.2 %copy.13 = bf16[1024,1024]{1,0:T(8,128)(2,1)} copy(bf16[1024,1024]{1,0:T(8,128)(2,1)} %get-tuple-element.8) | data formatting | bytes 4194304
  58.5 0.0 copy-done.2
  58.5 0.0 copy-start.1
  58.5 1.3 %copy.14 = bf16[1024,1024]{1,0:T(8,128)(2,1)} copy(bf16[1024,1024]{1,0:T(8,128)(2,1)S(1)} %copy-done.2) | data formatting | bytes 4194304
  59.8 1.0 %copy-done.1 = bf16[1024,1024]{1,0:T(8,128)(2,1)S(1)} copy-done((bf16[1024,1024]{1,0:T(8,128)(2,1)S(1)}, bf16[1024,1024]{1,0:T(8,128)(2,1)}, u32[]{:S(2)}) %copy-start.1) | copy-done | bytes 2097176
  60.9 0.0 copy-start
  60.9 1.3 %copy.15 = bf16[1024,1024]{1,0:T(8,128)(2,1)} copy(bf16[1024,1024]{1,0:T(8,128)(2,1)S(1)} %copy-done.1) | data formatting | bytes 4194304
  62.2 1.0 %copy-done = bf16[1024,1024]{1,0:T(8,128)(2,1)S(1)} copy-done((bf16[1024,1024]{1,0:T(8,128)(2,1)S(1)}, bf16[1024,1024]{1,0:T(8,128)(2,1)}, u32[]{:S(2)}) %copy-start) | copy-done | bytes 2097176
  63.2 1.3 %copy.16 = bf16[1024,1024]{1,0:T(8,128)(2,1)} copy(bf16[1024,1024]{1,0:T(8,128)(2,1)S(1)} %copy-done) | data formatting | bytes 4194304
Async XLA Ops:
  55.3 3.2 %copy-start.2 = (bf16[1024,1024]{1,0:T(8,128)(2,1)S(1)}, bf16[1024,1024]{1,0:T(8,128)(2,1)}, u32[]{:S(2)}) copy-start(bf16[1024,1024]{1,0:T(8,128)(2,1)} %get-tuple-element.9) | copy-start | bytes 6291460
  58.5 2.3 %copy-start.1 = (bf16[1024,1024]{1,0:T(8,128)(2,1)S(1)}, bf16[1024,1024]{1,0:T(8,128)(2,1)}, u32[]{:S(2)}) copy-start(bf16[1024,1024]{1,0:T(8,128)(2,1)} %get-tuple-element.10) | copy-start | bytes 6291460
  60.9 2.3 %copy-start = (bf16[1024,1024]{1,0:T(8,128)(2,1)S(1)}, bf16[1024,1024]{1,0:T(8,128)(2,1)}, u32[]{:S(2)}) copy-start(bf16[1024,1024]{1,0:T(8,128)(2,1)} %get-tuple-element.11) | copy-start | bytes 6291460

commit v2 on v1

--- a/solution.py
+++ b/solution.py
@@ -13,7 +13,7 @@
 HALF = 256
 D = H * HD
 TOK = 1024
-CHUNKS = 2
+CHUNKS = 4
 HPC = H // CHUNKS
 EPSILON = 1e-06
 F32 = jnp.float32
@@ -41,12 +41,12 @@
 
 def kernel(
     groups, shards,
-    q_hbm, k_hbm, v_hbm, gain_ref, dy_hbm,
-    no_hbm, gq_hbm, gk_hbm, gv_hbm,
-    qh, kh, vh, dyh, sc, att, ga, lk, lv, no_s, gq_s, gk_s, gv_s,
+    q_hbm, k_hbm, v_hbm, gain_hbm, dy_hbm,
+    no_ref, gq_ref, gk_ref, gv_ref,
+    qh, kh, vh, dyh, sc, att, ga, lk, lv,
     own, arrived, before, total, peers, result, inner, prior,
     squares, dots, inv_rows, mix_rows,
-    in_sem, out_sem, send_sem, recv_sem,
+    gain_ref, in_sem, gain_sem, send_sem, recv_sem,
 ):
     grp = lax.axis_index("grp")
     seq = lax.axis_index("seq")
@@ -60,11 +60,6 @@
         src = (k_hbm, v_hbm, q_hbm, dy_hbm)[i]
         dst = (kh, vh, qh, dyh)[i]
         return pltpu.make_async_copy(src.at[:, columns(h)], dst.at[h], in_sem.at[i, h])
-
-    def store(i, h):
-        src = (no_s, gq_s, gk_s, gv_s)[i]
-        dst = (no_hbm, gq_hbm, gk_hbm, gv_hbm)[i]
-        return pltpu.make_async_copy(src.at[h], dst.at[:, columns(h)], out_sem.at[i, h])
 
     def each(lo, hi, fn):
         def step(h, carry):
@@ -229,8 +224,7 @@
 
     def normed(h):
         gain = gain_ref[h]
-        no_s[h] = (att[h] * inv_rows[...] * gain).astype(BF16)
-        store(0, h).start()
+        no_ref[:, columns(h)] = (att[h] * inv_rows[...] * gain).astype(BF16)
 
     def backward(h):
         normed(h)
@@ -243,25 +237,21 @@
             s00 = causal(dot_nt(g0, v0)).astype(BF16)
             s10 = dot_nt(g1, v0).astype(BF16)
             s11 = causal(dot_nt(g1, v1)).astype(BF16)
-            gq_s[h, first(b, 0)] = (dot_nt(g0, p) + dot_nn(s00, k0)).astype(BF16)
-            gq_s[h, first(b, 1)] = (dot_nt(g1, p) + dot_nn(s10, k0) + dot_nn(s11, k1)).astype(BF16)
+            gq_ref[first(b, 0), columns(h)] = (dot_nt(g0, p) + dot_nn(s00, k0)).astype(BF16)
+            gq_ref[first(b, 1), columns(h)] = (dot_nt(g1, p) + dot_nn(s10, k0) + dot_nn(s11, k1)).astype(BF16)
             lk[h, first(b, 0)] = dot_tn(s00, q0) + dot_tn(s10, q1)
             lk[h, first(b, 1)] = dot_tn(s11, q1)
             lv[h, first(b, 0)] = dot_tn(sc[h, b, 0], g0) + dot_tn(sc[h, b, 1], g1)
             lv[h, first(b, 1)] = dot_tn(sc[h, b, 2], g1)
-        store(1, h).start()
 
     def finish(h):
         base = get_result(1, h)
         states = ((base + inner[1, h]).astype(BF16), base.astype(BF16))
         for b in range(2):
             rows = block(b)
-            gk_s[h, rows] = (lk[h, rows] + dot_nt(vh[h, rows], states[b])).astype(BF16)
-            gv_s[h, rows] = (lv[h, rows] + dot_nn(kh[h, rows], states[b])).astype(BF16)
-        store(2, h).start()
-        store(3, h).start()
-
-    start_loads((0, 1))
+            gk_ref[rows, columns(h)] = (lk[h, rows] + dot_nt(vh[h, rows], states[b])).astype(BF16)
+            gv_ref[rows, columns(h)] = (lv[h, rows] + dot_nn(kh[h, rows], states[b])).astype(BF16)
+
     barrier = pltpu.get_barrier_semaphore()
 
     def greet_seq(d):
@@ -276,75 +266,79 @@
 
     each(1, shards, greet_seq)
     each(1, groups, greet_grp)
+    start_loads((0, 1))
     start_loads((2, 3))
-
-    each(0, HPC, key_state)
-    pl.semaphore_wait(barrier, shards - 1 + groups - 1)
-    send_parts(0, 0)
-    each(HPC, H, key_state)
-    send_parts(0, 1)
+    gain_copy = pltpu.make_async_copy(gain_hbm, gain_ref, gain_sem)
+    gain_copy.start()
+
+    for c in range(CHUNKS):
+        each(c * HPC, (c + 1) * HPC, key_state)
+        if c == 0:
+            pl.semaphore_wait(barrier, shards - 1 + groups - 1)
+        send_parts(0, c)
 
     def wait_q(h):
         load(2, h).wait()
         load(3, h).wait()
 
     each(0, H, wait_q)
+    gain_copy.wait()
     squares[...] = jnp.zeros_like(squares)
     dots[...] = jnp.zeros_like(dots)
-    each(0, 4, local)
+    each(0, 6, local)
     scan_parts(0, 0)
-    each(4, 6, local)
+    each(6, 7, local)
     scan_parts(0, 1)
+    each(7, 8, local)
+    scan_parts(0, 2)
     return_parts(0, 0)
-    each(6, 8, local)
+    scan_parts(0, 3)
     return_parts(0, 1)
-    wait_result(0, 0)
-    each(0, HPC, attend)
-    wait_result(0, 1)
-    each(HPC, H, attend)
+    return_parts(0, 2)
+    return_parts(0, 3)
+    for c in range(CHUNKS):
+        wait_result(0, c)
+        each(c * HPC, (c + 1) * HPC, attend)
     row_factors()
-    each(0, HPC, grad_state)
-    send_parts(1, 0)
-    each(HPC, H, grad_state)
-    send_parts(1, 1)
+    for c in range(CHUNKS):
+        each(c * HPC, (c + 1) * HPC, grad_state)
+        send_parts(1, c)
     each(0, 3, backward)
     scan_parts(1, 0)
-    each(3, 5, backward)
+    each(3, 4, backward)
     scan_parts(1, 1)
+    each(4, 5, backward)
+    scan_parts(1, 2)
     return_parts(1, 0)
-    each(5, 8, backward)
+    each(5, 6, backward)
+    scan_parts(1, 3)
     return_parts(1, 1)
-    wait_result(1, 0)
-    each(0, HPC, finish)
-    wait_result(1, 1)
-    each(HPC, H, finish)
+    return_parts(1, 2)
+    return_parts(1, 3)
+    each(6, 8, backward)
+    for c in range(CHUNKS):
+        wait_result(1, c)
+        each(c * HPC, (c + 1) * HPC, finish)
     for w in range(2):
         for c in range(CHUNKS):
             wait_sends(w, c)
 
-    def wait_stores(h):
-        for i in range(4):
-            store(i, h).wait()
-
-    each(0, H, wait_stores)
-
 
 def body(groups, shards, queries, key_rows, value_rows, norm_gain, cotangent):
     sub = HPC * HD // shards
-    whole = jax.ShapeDtypeStruct((TOK, D), BF16)
-    anywhere = pl.BlockSpec(memory_space=pl.ANY)
+    whole = pltpu.VMEM((TOK, D), BF16)
+    anywhere = pl.BlockSpec(memory_space=pltpu.HBM)
     heads = lambda kind: pltpu.VMEM((H, TOK, HD), kind)
     parts = pltpu.VMEM((2, CHUNKS, shards, sub, HD), F32)
     return tuple(pl.pallas_call(
         functools.partial(kernel, groups, shards),
         out_shape=(whole,) * 4,
-        in_specs=[anywhere, anywhere, anywhere, pl.BlockSpec(memory_space=pltpu.VMEM), anywhere],
-        out_specs=(anywhere,) * 4,
+        in_specs=[anywhere] * 5,
+        out_specs=(pl.BlockSpec(memory_space=pltpu.VMEM),) * 4,
         scratch_shapes=[
             heads(BF16), heads(BF16), heads(BF16), heads(BF16),
             pltpu.VMEM((H, 2, 3, HALF, HALF), BF16),
             heads(F32), heads(BF16), heads(F32), heads(F32),
-            heads(BF16), heads(BF16), heads(BF16), heads(BF16),
             parts, parts, parts,
             pltpu.VMEM((2, CHUNKS, sub, HD), F32),
             pltpu.VMEM((2, CHUNKS, groups, sub, HD), F32),
@@ -353,13 +347,14 @@
             pltpu.VMEM((H, 2, HD, HD), BF16),
             pltpu.VMEM((TOK, HD), F32), pltpu.VMEM((TOK, HD), F32),
             pltpu.VMEM((TOK, HD), F32), pltpu.VMEM((TOK, HD), F32),
+            pltpu.VMEM((H, 1, HD), F32),
             pltpu.SemaphoreType.DMA((4, H)),
-            pltpu.SemaphoreType.DMA((4, H)),
+            pltpu.SemaphoreType.DMA,
             pltpu.SemaphoreType.DMA((2, CHUNKS, 3)),
             pltpu.SemaphoreType.DMA((2, CHUNKS, 3)),
         ],
         compiler_params=pltpu.CompilerParams(
-            collective_id=0, has_side_effects=True, vmem_limit_bytes=60 * 1024 * 1024
+            collective_id=0, has_side_effects=True, vmem_limit_bytes=40 * 1024 * 1024
         ),
         name="attention",
     )(queries, key_rows, value_rows, norm_gain.reshape(H, 1, HD), cotangent))

time: 64.7 us -> 60.5 us (0.935)
  Pallas kernels: 54.6 us -> 50.5 us
    pallas_call x1, Pallas kernels: 54.6 us -> 50.5 us  [body(): pl.pallas_call(functools.partial(kernel, groups, shards), out_shape=(whol...]
where the time goes in v2:
time: 60.5 us; the launch traced here: 60.3 us
  Pallas kernels  50.5 us (83%)
  local copies, waits for them, and re-layouts  9.14 us (15%)
  between operations  0.65 us (1%)
    pallas_call x1, Pallas kernels, body(): pl.pallas_call(functools.partial(kernel, groups, shards), out_shape=(whol...  50.5 us
    unnamed x10, local copies, waits for them, and re-layouts  9.14 us

profile of v2, /device:TPU:1, one launch (start us, length us, event | category | flops | bytes accessed | tf_op | source)
XLA Modules:
  0.0 60.3 jit_solution(5979273393618646084)
XLA Ops:
  0.6 0.0 copy-start
  0.6 1.6 %copy-done = bf16[1024,1024]{1,0:T(8,128)(2,1)S(1)} copy-done((bf16[1024,1024]{1,0:T(8,128)(2,1)S(1)}, bf16[1024,1024]{1,0:T(8,128)(2,1)}, u32[]{:S(2)}) %copy-start) | copy-done | bytes 2097176
  2.2 0.0 copy-start.1
  2.2 1.6 %copy-done.1 = bf16[1024,1024]{1,0:T(8,128)(2,1)S(1)} copy-done((bf16[1024,1024]{1,0:T(8,128)(2,1)S(1)}, bf16[1024,1024]{1,0:T(8,128)(2,1)}, u32[]{:S(2)}) %copy-start.1) | copy-done | bytes 2097176
  3.8 0.0 copy-start.2
  3.8 0.7 %copy-done.2 = f32[1024]{0:T(1024)S(1)} copy-done((f32[1024]{0:T(1024)S(1)}, f32[1024]{0:T(1024)}, u32[]{:S(2)}) %copy-start.2) | copy-done | bytes 4120
  4.5 50.5 %attention.1 = (bf16[1024,1024]{1,0:T(8,128)(2,1)S(1)}, bf16[1024,1024]{1,0:T(8,128)(2,1)S(1)}, bf16[1024,1024]{1,0:T(8,128)(2,1)S(1)}, bf16[1024,1024]{1,0:T(8,128)(2,1)S(1)}) custom-call(bf16[1024,1024]{1,0:T(8,128)(2,1)S(1)} %copy-done, bf16[1024,1024]{1,0:T(8,128)(2,1)S(1)} %copy-done.1, bf16[1024,1024]{1,0:T(8,128)(2,1)} %v_hbm.1, ...), custom_call_target="tpu_custom_call" | custom-call | tf_op jit(solution)/shard_map/attention/pallas_call | solution.py:333
  55.0 1.3 %copy.13 = bf16[1024,1024]{1,0:T(8,128)(2,1)} copy(bf16[1024,1024]{1,0:T(8,128)(2,1)S(1)} %get-tuple-element.4) | data formatting | bytes 4194304
  56.3 1.3 %copy.14 = bf16[1024,1024]{1,0:T(8,128)(2,1)} copy(bf16[1024,1024]{1,0:T(8,128)(2,1)S(1)} %get-tuple-element.5) | data formatting | bytes 4194304
  57.6 1.3 %copy.15 = bf16[1024,1024]{1,0:T(8,128)(2,1)} copy(bf16[1024,1024]{1,0:T(8,128)(2,1)S(1)} %get-tuple-element.6) | data formatting | bytes 4194304
  58.9 1.3 %copy.16 = bf16[1024,1024]{1,0:T(8,128)(2,1)} copy(bf16[1024,1024]{1,0:T(8,128)(2,1)S(1)} %get-tuple-element.7) | data formatting | bytes 4194304
Async XLA Ops:
  0.6 1.6 %copy-start = (bf16[1024,1024]{1,0:T(8,128)(2,1)S(1)}, bf16[1024,1024]{1,0:T(8,128)(2,1)}, u32[]{:S(2)}) copy-start(bf16[1024,1024]{1,0:T(8,128)(2,1)} %q_hbm.1) | copy-start | bytes 6291460
  2.2 1.6 %copy-start.1 = (bf16[1024,1024]{1,0:T(8,128)(2,1)S(1)}, bf16[1024,1024]{1,0:T(8,128)(2,1)}, u32[]{:S(2)}) copy-start(bf16[1024,1024]{1,0:T(8,128)(2,1)} %k_hbm.1) | copy-start | bytes 6291460
  3.8 0.7 %copy-start.2 = (f32[1024]{0:T(1024)S(1)}, f32[1024]{0:T(1024)}, u32[]{:S(2)}) copy-start(f32[1024]{0:T(1024)} %param.8) | copy-start | bytes 12292

commit v3 on v2

--- a/solution.py
+++ b/solution.py
@@ -15,6 +15,7 @@
 TOK = 1024
 CHUNKS = 4
 HPC = H // CHUNKS
+PIECES = 2
 EPSILON = 1e-06
 F32 = jnp.float32
 BF16 = jnp.bfloat16
@@ -53,6 +54,20 @@
     sub = HPC * HD // shards
     per_head = HD // sub
 
+    def ring(step):
+        return min(step, 4 - step)
+
+    offsets = [(dz, dx) for dz in range(shards // 4) for dx in range(4) if dz or dx]
+    offsets.sort(key=lambda o: -ring(o[0]) - ring(o[1]))
+    shard_peers = [
+        lax.rem(seq // 4 + dz, shards // 4) * 4 + lax.rem(seq % 4 + dx, 4) for dz, dx in offsets
+    ]
+    offsets = [(dy, dc) for dy in range(groups // 2) for dc in range(2) if dy or dc]
+    offsets.sort(key=lambda o: -ring(o[0]) * 2 - o[1])
+    group_peers = [
+        lax.rem(grp // 2 + dy, groups // 2) * 2 + lax.rem(grp % 2 + dc, 2) for dy, dc in offsets
+    ]
+
     def columns(h):
         return pl.ds(pl.multiple_of(h * HD, HD), HD)
 
@@ -74,14 +89,12 @@
         each(0, H, one)
 
     def send_parts(w, c):
-        def one(d):
-            to = lax.rem(seq + d, shards)
+        for to in shard_peers:
             pltpu.make_async_remote_copy(
                 own.at[w, c, to], arrived.at[w, c, seq],
                 send_sem.at[w, c, 0], recv_sem.at[w, c, 0],
                 device_id=(grp, to), device_id_type=MESH,
             ).start()
-        each(1, shards, one)
         arrived[w, c, seq] = own[w, c, seq]
 
     def wait_parts(w, c):
@@ -100,14 +113,12 @@
             running = running + arrived[w, c, t]
         total[w, c] = running
 
-        def one(d):
-            to = lax.rem(grp + d, groups)
+        for to in group_peers:
             pltpu.make_async_remote_copy(
                 total.at[w, c], peers.at[w, c, grp],
                 send_sem.at[w, c, 1], recv_sem.at[w, c, 1],
                 device_id=(to, seq), device_id_type=MESH,
             ).start()
-        each(1, groups, one)
 
     def return_parts(w, c):
         pltpu.make_async_remote_copy(
@@ -122,14 +133,12 @@
         for t in range(shards):
             before[w, c, t] = before[w, c, t] + base
 
-        def one(d):
-            to = lax.rem(seq + d, shards)
+        for to in shard_peers:
             pltpu.make_async_remote_copy(
                 before.at[w, c, to], result.at[w, c, seq],
                 send_sem.at[w, c, 2], recv_sem.at[w, c, 2],
                 device_id=(grp, to), device_id_type=MESH,
             ).start()
-        each(1, shards, one)
         result[w, c, seq] = before[w, c, seq]
 
     def wait_result(w, c):
@@ -254,18 +263,10 @@
 
     barrier = pltpu.get_barrier_semaphore()
 
-    def greet_seq(d):
-        pl.semaphore_signal(
-            barrier, inc=1, device_id=(grp, lax.rem(seq + d, shards)), device_id_type=MESH
-        )
-
-    def greet_grp(d):
-        pl.semaphore_signal(
-            barrier, inc=1, device_id=(lax.rem(grp + d, groups), seq), device_id_type=MESH
-        )
-
-    each(1, shards, greet_seq)
-    each(1, groups, greet_grp)
+    for to in shard_peers:
+        pl.semaphore_signal(barrier, inc=1, device_id=(grp, to), device_id_type=MESH)
+    for to in group_peers:
+        pl.semaphore_signal(barrier, inc=1, device_id=(to, seq), device_id_type=MESH)
     start_loads((0, 1))
     start_loads((2, 3))
     gain_copy = pltpu.make_async_copy(gain_hbm, gain_ref, gain_sem)
@@ -330,7 +331,7 @@
     anywhere = pl.BlockSpec(memory_space=pltpu.HBM)
     heads = lambda kind: pltpu.VMEM((H, TOK, HD), kind)
     parts = pltpu.VMEM((2, CHUNKS, shards, sub, HD), F32)
-    return tuple(pl.pallas_call(
+    return tuple(write_out(pl.pallas_call(
         functools.partial(kernel, groups, shards),
         out_shape=(whole,) * 4,
         in_specs=[anywhere] * 5,
@@ -354,10 +355,35 @@
             pltpu.SemaphoreType.DMA((2, CHUNKS, 3)),
         ],
         compiler_params=pltpu.CompilerParams(
-            collective_id=0, has_side_effects=True, vmem_limit_bytes=40 * 1024 * 1024
+            collective_id=0, has_side_effects=True, vmem_limit_bytes=50 * 1024 * 1024
         ),
         name="attention",
-    )(queries, key_rows, value_rows, norm_gain.reshape(H, 1, HD), cotangent))
+    )(queries, key_rows, value_rows, norm_gain.reshape(H, 1, HD), cotangent)))
+
+
+def write_kernel(a, b, c, d, ao, bo, co, do, sems):
+    copies = []
+    for i, (src, dst) in enumerate(((a, ao), (b, bo), (c, co), (d, do))):
+        for j in range(PIECES):
+            rows = pl.ds(j * (TOK // PIECES), TOK // PIECES)
+            copies.append(pltpu.make_async_copy(src.at[rows], dst.at[rows], sems.at[i, j]))
+    for copy in copies:
+        copy.start()
+    for copy in copies:
+        copy.wait()
+
+
+def write_out(arrays):
+    whole = jax.ShapeDtypeStruct((TOK, D), BF16)
+    return pl.pallas_call(
+        write_kernel,
+        out_shape=(whole,) * 4,
+        in_specs=[pl.BlockSpec(memory_space=pl.ANY)] * 4,
+        out_specs=(pl.BlockSpec(memory_space=pltpu.HBM),) * 4,
+        scratch_shapes=[pltpu.SemaphoreType.DMA((4, PIECES))],
+        compiler_params=pltpu.CompilerParams(vmem_limit_bytes=1024 * 1024),
+        name="write_out",
+    )(*(pltpu.with_memory_space_constraint(a, pltpu.VMEM) for a in arrays))
 
 
 def solution(mesh):

time: 60.5 us -> 53.2 us (0.88)
  local copies, waits for them, and re-layouts: 9.14 us -> 0 us
  Pallas kernels: 50.5 us -> 52.4 us
    unnamed x10 -> x0, local copies, waits for them, and re-layouts: 9.14 us -> none
    pallas_call x0 -> x1, Pallas kernels: none -> 3.37 us  [write_out(): pl.pallas_call(write_kernel, out_shape=(whole,) * 4, in_specs=[pl.BlockSp...]
    pallas_call x1, Pallas kernels: 50.5 us -> 49 us  [body(): pl.pallas_call(functools.partial(kernel, groups, shards), out_shape=(whol...]
where the time goes in v3:
time: 53.2 us; the launch traced here: 53.1 us
  Pallas kernels  52.4 us (98%)
  between operations  0.64 us (1%)
    pallas_call x1, Pallas kernels, body(): pl.pallas_call(functools.partial(kernel, groups, shards), out_shape=(whol...  49 us
    pallas_call x1, Pallas kernels, write_out(): pl.pallas_call(write_kernel, out_shape=(whole,) * 4, in_specs=[pl.BlockSp...  3.37 us

profile of v3, /device:TPU:1, one launch (start us, length us, event | category | flops | bytes accessed | tf_op | source)
XLA Modules:
  0.0 53.1 jit_solution(16416415798756566414)
XLA Ops:
  0.6 49.0 %attention.1 = (bf16[1024,1024]{1,0:T(8,128)(2,1)S(1)}, bf16[1024,1024]{1,0:T(8,128)(2,1)S(1)}, bf16[1024,1024]{1,0:T(8,128)(2,1)S(1)}, bf16[1024,1024]{1,0:T(8,128)(2,1)S(1)}) custom-call(bf16[1024,1024]{1,0:T(8,128)(2,1)} %q_hbm.1, bf16[1024,1024]{1,0:T(8,128)(2,1)} %k_hbm.1, bf16[1024,1024]{1,0:T(8,128)(2,1)} %v_hbm.1, f32[8,1,128]{2,1,0:T(1,128)} %bitcast.1, ...), custom_call_target="tpu_custom_call" | custom-call | tf_op jit(solution)/shard_map/attention/pallas_call | solution.py:334
  49.7 3.4 %write_out.1 = (bf16[1024,1024]{1,0:T(8,128)(2,1)}, bf16[1024,1024]{1,0:T(8,128)(2,1)}, bf16[1024,1024]{1,0:T(8,128)(2,1)}, bf16[1024,1024]{1,0:T(8,128)(2,1)}) custom-call(bf16[1024,1024]{1,0:T(8,128)(2,1)S(1)} %get-tuple-element.8.a, bf16[1024,1024]{1,0:T(8,128)(2,1)S(1)} %get-tuple-element.9.b, bf16[1024,1024]{1,0:T(8,128)(2,1)S(1)} %get-tuple-element.10.c, ...), custom_call_target="tpu_custom_call" | custom-call | tf_op jit(solution)/shard_map/write_out/pallas_call | solution.py:378

commit v4 on v3

--- a/solution.py
+++ b/solution.py
@@ -13,9 +13,15 @@
 HALF = 256
 D = H * HD
 TOK = 1024
-CHUNKS = 4
-HPC = H // CHUNKS
+BOUNDS = (0, 1, 3, 5, 7, 8)
+CHUNKS = len(BOUNDS) - 1
 PIECES = 2
+FORWARD = (
+    ("h", 3), ("s", 0), ("h", 1), ("s", 1), ("h", 1), ("s", 2), ("r", 0), ("s", 3), ("s", 4), ("r", 1), ("h", 1), ("r", 2), ("r", 3), ("r", 4), ("h", 2),
+)
+BACKWARD = (
+    ("h", 2), ("s", 0), ("h", 1), ("s", 1), ("h", 1), ("s", 2), ("r", 0), ("s", 3), ("s", 4), ("r", 1), ("h", 1), ("r", 2), ("r", 3), ("r", 4), ("h", 3),
+)
 EPSILON = 1e-06
 F32 = jnp.float32
 BF16 = jnp.bfloat16
@@ -40,19 +46,27 @@
     return jnp.where(rows >= cols, tile, 0.0)
 
 
+def causal_t(tile):
+    rows = lax.broadcasted_iota(jnp.int32, tile.shape, 0)
+    cols = lax.broadcasted_iota(jnp.int32, tile.shape, 1)
+    return jnp.where(cols >= rows, tile, 0.0)
+
+
 def kernel(
     groups, shards,
     q_hbm, k_hbm, v_hbm, gain_hbm, dy_hbm,
     no_ref, gq_ref, gk_ref, gv_ref,
-    qh, kh, vh, dyh, sc, att, ga, lk, lv,
+    qh, kh, vh, dyh, qt, sc, att, ga, lk, lv,
     own, arrived, before, total, peers, result, inner, prior,
     squares, dots, inv_rows, mix_rows,
     gain_ref, in_sem, gain_sem, send_sem, recv_sem,
 ):
     grp = lax.axis_index("grp")
     seq = lax.axis_index("seq")
-    sub = HPC * HD // shards
-    per_head = HD // sub
+    sub = HD // shards
+
+    def span(c):
+        return pl.ds(BOUNDS[c], BOUNDS[c + 1] - BOUNDS[c])
 
     def ring(step):
         return min(step, 4 - step)
@@ -88,83 +102,62 @@
                 load(i, h).start()
         each(0, H, one)
 
+    def sent(w, c, phase, src, dst, device):
+        return pltpu.make_async_remote_copy(
+            src, dst, send_sem.at[w, c, phase], recv_sem.at[w, c, phase],
+            device_id=device, device_id_type=MESH,
+        )
+
+    def all_of(w, c, phase):
+        ref, count = ((own, shards), (peers, groups), (before, shards))[phase]
+        part = ref.at[w, span(c), pl.ds(0, count - 1)]
+        return sent(w, c, phase, part, part, (grp, seq))
+
     def send_parts(w, c):
         for to in shard_peers:
-            pltpu.make_async_remote_copy(
-                own.at[w, c, to], arrived.at[w, c, seq],
-                send_sem.at[w, c, 0], recv_sem.at[w, c, 0],
-                device_id=(grp, to), device_id_type=MESH,
-            ).start()
-        arrived[w, c, seq] = own[w, c, seq]
-
-    def wait_parts(w, c):
-        pltpu.make_async_remote_copy(
-            own.at[w, c, pl.ds(0, shards - 1)], arrived.at[w, c, pl.ds(0, shards - 1)],
-            send_sem.at[w, c, 0], recv_sem.at[w, c, 0],
-            device_id=(grp, seq), device_id_type=MESH,
-        ).wait_recv()
+            sent(w, c, 0, own.at[w, span(c), to], arrived.at[w, span(c), seq], (grp, to)).start()
+        arrived[w, span(c), seq] = own[w, span(c), seq]
 
     def scan_parts(w, c):
-        wait_parts(w, c)
+        all_of(w, c, 0).wait_recv()
         order = range(shards) if w == 0 else range(shards - 1, -1, -1)
-        running = jnp.zeros((sub, HD), F32)
-        for t in order:
-            before[w, c, t] = running
-            running = running + arrived[w, c, t]
-        total[w, c] = running
-
+        parts = [arrived[w, span(c), t] for t in order]
+        sums = parts
+        while len(sums) > 1:
+            sums = [sums[i] + sums[i + 1] for i in range(0, len(sums), 2)]
+        total[w, span(c)] = sums[0]
         for to in group_peers:
-            pltpu.make_async_remote_copy(
-                total.at[w, c], peers.at[w, c, grp],
-                send_sem.at[w, c, 1], recv_sem.at[w, c, 1],
-                device_id=(to, seq), device_id_type=MESH,
-            ).start()
+            sent(w, c, 1, total.at[w, span(c)], peers.at[w, span(c), grp], (to, seq)).start()
+        peers[w, span(c), grp] = sums[0]
+        running = jnp.zeros_like(sums[0])
+        for t, part in zip(order, parts):
+            before[w, span(c), t] = running
+            running = running + part
 
     def return_parts(w, c):
-        pltpu.make_async_remote_copy(
-            peers.at[w, c, pl.ds(0, groups - 1)], peers.at[w, c, pl.ds(0, groups - 1)],
-            send_sem.at[w, c, 1], recv_sem.at[w, c, 1],
-            device_id=(grp, seq), device_id_type=MESH,
-        ).wait_recv()
-        lo, hi = (0, grp) if w == 0 else (grp + 1, groups)
-        base = lax.fori_loop(
-            lo, hi, lambda g, s: s + peers[w, c, g], jnp.zeros((sub, HD), F32)
-        )
+        all_of(w, c, 1).wait_recv()
+        base = jnp.zeros((BOUNDS[c + 1] - BOUNDS[c], sub, HD), F32)
+        for g in range(groups):
+            inside = g < grp if w == 0 else g > grp
+            base = base + jnp.where(inside, peers[w, span(c), g], 0.0)
         for t in range(shards):
-            before[w, c, t] = before[w, c, t] + base
-
+            before[w, span(c), t] = before[w, span(c), t] + base
         for to in shard_peers:
-            pltpu.make_async_remote_copy(
-                before.at[w, c, to], result.at[w, c, seq],
-                send_sem.at[w, c, 2], recv_sem.at[w, c, 2],
-                device_id=(grp, to), device_id_type=MESH,
-            ).start()
-        result[w, c, seq] = before[w, c, seq]
+            sent(w, c, 2, before.at[w, span(c), to], result.at[w, span(c), seq], (grp, to)).start()
+        result[w, span(c), seq] = before[w, span(c), seq]
 
     def wait_result(w, c):
-        pltpu.make_async_remote_copy(
-            before.at[w, c, pl.ds(0, shards - 1)], result.at[w, c, pl.ds(0, shards - 1)],
-            send_sem.at[w, c, 2], recv_sem.at[w, c, 2],
-            device_id=(grp, seq), device_id_type=MESH,
-        ).wait_recv()
+        all_of(w, c, 2).wait_recv()
 
     def wait_sends(w, c):
-        for phase, ref, count in ((0, own, shards), (1, peers, groups), (2, before, shards)):
-            pltpu.make_async_remote_copy(
-                ref.at[w, c, pl.ds(0, count - 1)], ref.at[w, c, pl.ds(0, count - 1)],
-                send_sem.at[w, c, phase], recv_sem.at[w, c, phase],
-                device_id=(grp, seq), device_id_type=MESH,
-            ).wait_send()
+        for phase in range(3):
+            all_of(w, c, phase).wait_send()
 
     def put_own(w, h, value):
-        c = h // HPC
-        at = pl.multiple_of((h % HPC) * per_head, per_head)
-        own[w, c, pl.ds(at, per_head)] = value.reshape(per_head, sub, HD)
+        own[w, h] = value.reshape(shards, sub, HD)
 
     def get_result(w, h):
-        c = h // HPC
-        at = pl.multiple_of((h % HPC) * per_head, per_head)
-        return result[w, c, pl.ds(at, per_head)].reshape(HD, HD)
+        return result[w, h].reshape(HD, HD)
 
     def first(b, i):
         return pl.ds(b * BLOCK + i * HALF, HALF)
@@ -188,9 +181,10 @@
             t00 = causal(dot_nt(q0, k0)).astype(BF16)
             t10 = dot_nt(q1, k0).astype(BF16)
             t11 = causal(dot_nt(q1, k1)).astype(BF16)
-            sc[h, b, 0] = t00
-            sc[h, b, 1] = t10
-            sc[h, b, 2] = t11
+            sc[h, b, 0] = causal_t(dot_nt(k0, q0)).astype(BF16)
+            sc[h, b, 1] = dot_nt(k0, q1).astype(BF16)
+            sc[h, b, 2] = causal_t(dot_nt(k1, q1)).astype(BF16)
+            qt[h, :, block(b)] = jnp.transpose(qh[h, block(b)])
             att[h, first(b, 0)] = dot_nn(t00, v0)
             att[h, first(b, 1)] = dot_nn(t10, v0) + dot_nn(t11, v1)
 
@@ -227,7 +221,7 @@
             scaled = dyh[h, rows].astype(F32) * gain
             grad = (inv_rows[rows] * scaled - mix_rows[rows] * att[h, rows]).astype(BF16)
             ga[h, rows] = grad
-            parts.append(dot_tn(qh[h, rows], grad))
+            parts.append(dot_nn(qt[h, :, rows], grad))
         inner[1, h] = parts[1]
         put_own(1, h, parts[0] + parts[1])
 
@@ -238,7 +232,7 @@
     def backward(h):
         normed(h)
         for b in range(2):
-            q0, q1 = qh[h, first(b, 0)], qh[h, first(b, 1)]
+            q0, q1 = qt[h, :, first(b, 0)], qt[h, :, first(b, 1)]
             k0, k1 = kh[h, first(b, 0)], kh[h, first(b, 1)]
             v0, v1 = vh[h, first(b, 0)], vh[h, first(b, 1)]
             g0, g1 = ga[h, first(b, 0)], ga[h, first(b, 1)]
@@ -248,10 +242,10 @@
             s11 = causal(dot_nt(g1, v1)).astype(BF16)
             gq_ref[first(b, 0), columns(h)] = (dot_nt(g0, p) + dot_nn(s00, k0)).astype(BF16)
             gq_ref[first(b, 1), columns(h)] = (dot_nt(g1, p) + dot_nn(s10, k0) + dot_nn(s11, k1)).astype(BF16)
-            lk[h, first(b, 0)] = dot_tn(s00, q0) + dot_tn(s10, q1)
-            lk[h, first(b, 1)] = dot_tn(s11, q1)
-            lv[h, first(b, 0)] = dot_tn(sc[h, b, 0], g0) + dot_tn(sc[h, b, 1], g1)
-            lv[h, first(b, 1)] = dot_tn(sc[h, b, 2], g1)
+            lk[h, first(b, 0)] = jnp.transpose(dot_nn(q0, s00) + dot_nn(q1, s10))
+            lk[h, first(b, 1)] = jnp.transpose(dot_nn(q1, s11))
+            lv[h, first(b, 0)] = dot_nn(sc[h, b, 0], g0) + dot_nn(sc[h, b, 1], g1)
+            lv[h, first(b, 1)] = dot_nn(sc[h, b, 2], g1)
 
     def finish(h):
         base = get_result(1, h)
@@ -268,15 +262,15 @@
     for to in group_peers:
         pl.semaphore_signal(barrier, inc=1, device_id=(to, seq), device_id_type=MESH)
     start_loads((0, 1))
-    start_loads((2, 3))
-    gain_copy = pltpu.make_async_copy(gain_hbm, gain_ref, gain_sem)
-    gain_copy.start()
-
     for c in range(CHUNKS):
-        each(c * HPC, (c + 1) * HPC, key_state)
+        each(BOUNDS[c], BOUNDS[c + 1], key_state)
         if c == 0:
             pl.semaphore_wait(barrier, shards - 1 + groups - 1)
         send_parts(0, c)
+        if c == 0:
+            start_loads((2, 3))
+            gain_copy = pltpu.make_async_copy(gain_hbm, gain_ref, gain_sem)
+            gain_copy.start()
 
     def wait_q(h):
         load(2, h).wait()
@@ -286,51 +280,40 @@
     gain_copy.wait()
     squares[...] = jnp.zeros_like(squares)
     dots[...] = jnp.zeros_like(dots)
-    each(0, 6, local)
-    scan_parts(0, 0)
-    each(6, 7, local)
-    scan_parts(0, 1)
-    each(7, 8, local)
-    scan_parts(0, 2)
-    return_parts(0, 0)
-    scan_parts(0, 3)
-    return_parts(0, 1)
-    return_parts(0, 2)
-    return_parts(0, 3)
+    def run(plan, w, work):
+        done = 0
+        for kind, n in plan:
+            if kind == "s":
+                scan_parts(w, n)
+            elif kind == "r":
+                return_parts(w, n)
+            else:
+                each(done, done + n, work)
+                done += n
+
+    run(FORWARD, 0, local)
     for c in range(CHUNKS):
         wait_result(0, c)
-        each(c * HPC, (c + 1) * HPC, attend)
+        each(BOUNDS[c], BOUNDS[c + 1], attend)
     row_factors()
     for c in range(CHUNKS):
-        each(c * HPC, (c + 1) * HPC, grad_state)
+        each(BOUNDS[c], BOUNDS[c + 1], grad_state)
         send_parts(1, c)
-    each(0, 3, backward)
-    scan_parts(1, 0)
-    each(3, 4, backward)
-    scan_parts(1, 1)
-    each(4, 5, backward)
-    scan_parts(1, 2)
-    return_parts(1, 0)
-    each(5, 6, backward)
-    scan_parts(1, 3)
-    return_parts(1, 1)
-    return_parts(1, 2)
-    return_parts(1, 3)
-    each(6, 8, backward)
+    run(BACKWARD, 1, backward)
     for c in range(CHUNKS):
         wait_result(1, c)
-        each(c * HPC, (c + 1) * HPC, finish)
+        each(BOUNDS[c], BOUNDS[c + 1], finish)
     for w in range(2):
         for c in range(CHUNKS):
             wait_sends(w, c)
 
 
 def body(groups, shards, queries, key_rows, value_rows, norm_gain, cotangent):
-    sub = HPC * HD // shards
+    sub = HD // shards
     whole = pltpu.VMEM((TOK, D), BF16)
     anywhere = pl.BlockSpec(memory_space=pltpu.HBM)
     heads = lambda kind: pltpu.VMEM((H, TOK, HD), kind)
-    parts = pltpu.VMEM((2, CHUNKS, shards, sub, HD), F32)
+    parts = pltpu.VMEM((2, H, shards, sub, HD), F32)
     return tuple(write_out(pl.pallas_call(
         functools.partial(kernel, groups, shards),
         out_shape=(whole,) * 4,
@@ -338,11 +321,12 @@
         out_specs=(pl.BlockSpec(memory_space=pltpu.VMEM),) * 4,
         scratch_shapes=[
             heads(BF16), heads(BF16), heads(BF16), heads(BF16),
+            pltpu.VMEM((H, HD, TOK), BF16),
             pltpu.VMEM((H, 2, 3, HALF, HALF), BF16),
             heads(F32), heads(BF16), heads(F32), heads(F32),
             parts, parts, parts,
-            pltpu.VMEM((2, CHUNKS, sub, HD), F32),
-            pltpu.VMEM((2, CHUNKS, groups, sub, HD), F32),
+            pltpu.VMEM((2, H, sub, HD), F32),
+            pltpu.VMEM((2, H, groups, sub, HD), F32),
             parts,
             pltpu.VMEM((2, H, HD, HD), F32),
             pltpu.VMEM((H, 2, HD, HD), BF16),

time: 53.2 us -> 51.2 us (0.962)
  Pallas kernels: 52.4 us -> 50.3 us
    pallas_call x1, Pallas kernels: 49 us -> 47 us  [body(): pl.pallas_call(functools.partial(kernel, groups, shards), out_shape=(whol...]
where the time goes in v4:
time: 51.2 us; the launch traced here: 51.1 us
  Pallas kernels  50.3 us (98%)
  between operations  0.8 us (2%)
    pallas_call x1, Pallas kernels, body(): pl.pallas_call(functools.partial(kernel, groups, shards), out_shape=(whol...  47 us
    pallas_call x1, Pallas kernels, write_out(): pl.pallas_call(write_kernel, out_shape=(whole,) * 4, in_specs=[pl.BlockSp...  3.37 us

profile of v4, /device:TPU:1, one launch (start us, length us, event | category | flops | bytes accessed | tf_op | source)
XLA Modules:
  0.0 51.1 jit_solution(17331415036702109783)
XLA Ops:
  0.6 47.0 %attention.1 = (bf16[1024,1024]{1,0:T(8,128)(2,1)S(1)}, bf16[1024,1024]{1,0:T(8,128)(2,1)S(1)}, bf16[1024,1024]{1,0:T(8,128)(2,1)S(1)}, bf16[1024,1024]{1,0:T(8,128)(2,1)S(1)}) custom-call(bf16[1024,1024]{1,0:T(8,128)(2,1)} %q_hbm.1, bf16[1024,1024]{1,0:T(8,128)(2,1)} %k_hbm.1, bf16[1024,1024]{1,0:T(8,128)(2,1)} %v_hbm.1, f32[8,1,128]{2,1,0:T(1,128)} %bitcast.1, ...), custom_call_target="tpu_custom_call" | custom-call | tf_op jit(solution)/shard_map/attention/pallas_call | solution.py:317
  47.6 3.4 %write_out.1 = (bf16[1024,1024]{1,0:T(8,128)(2,1)}, bf16[1024,1024]{1,0:T(8,128)(2,1)}, bf16[1024,1024]{1,0:T(8,128)(2,1)}, bf16[1024,1024]{1,0:T(8,128)(2,1)}) custom-call(bf16[1024,1024]{1,0:T(8,128)(2,1)S(1)} %get-tuple-element.8.a, bf16[1024,1024]{1,0:T(8,128)(2,1)S(1)} %get-tuple-element.9.b, bf16[1024,1024]{1,0:T(8,128)(2,1)S(1)} %get-tuple-element.10.c, ...), custom_call_target="tpu_custom_call" | custom-call | tf_op jit(solution)/shard_map/write_out/pallas_call | solution.py:362

commit v5 on v4

--- a/solution.py
+++ b/solution.py
@@ -91,6 +91,10 @@
         return pltpu.make_async_copy(src.at[:, columns(h)], dst.at[h], in_sem.at[i, h])
 
     def each(lo, hi, fn):
+        if hi - lo == 1:
+            fn(lo)
+            return
+
         def step(h, carry):
             fn(h)
             return carry
@@ -174,6 +178,7 @@
         put_own(0, h, s0 + s1)
 
     def local(h):
+        load(2, h).wait()
         for b in range(2):
             q0, q1 = qh[h, first(b, 0)], qh[h, first(b, 1)]
             k0, k1 = kh[h, first(b, 0)], kh[h, first(b, 1)]
@@ -272,12 +277,6 @@
             gain_copy = pltpu.make_async_copy(gain_hbm, gain_ref, gain_sem)
             gain_copy.start()
 
-    def wait_q(h):
-        load(2, h).wait()
-        load(3, h).wait()
-
-    each(0, H, wait_q)
-    gain_copy.wait()
     squares[...] = jnp.zeros_like(squares)
     dots[...] = jnp.zeros_like(dots)
     def run(plan, w, work):
@@ -292,6 +291,8 @@
                 done += n
 
     run(FORWARD, 0, local)
+    each(0, H, lambda h: load(3, h).wait())
+    gain_copy.wait()
     for c in range(CHUNKS):
         wait_result(0, c)
         each(BOUNDS[c], BOUNDS[c + 1], attend)

time: 51.2 us -> 51 us (level)
  no operation moved by 1% of the time
where the time goes in v5:
time: 51 us; the launch traced here: 50.9 us
  Pallas kernels  50.1 us (98%)
  between operations  0.8 us (2%)
    pallas_call x1, Pallas kernels, body(): pl.pallas_call(functools.partial(kernel, groups, shards), out_shape=(whol...  46.8 us
    pallas_call x1, Pallas kernels, write_out(): pl.pallas_call(write_kernel, out_shape=(whole,) * 4, in_specs=[pl.BlockSp...  3.37 us

profile of v5, /device:TPU:1, one launch (start us, length us, event | category | flops | bytes accessed | tf_op | source)
XLA Modules:
  0.0 50.9 jit_solution(14338823347916700913)
XLA Ops:
  0.6 46.8 %attention.1 = (bf16[1024,1024]{1,0:T(8,128)(2,1)S(1)}, bf16[1024,1024]{1,0:T(8,128)(2,1)S(1)}, bf16[1024,1024]{1,0:T(8,128)(2,1)S(1)}, bf16[1024,1024]{1,0:T(8,128)(2,1)S(1)}) custom-call(bf16[1024,1024]{1,0:T(8,128)(2,1)} %q_hbm.1, bf16[1024,1024]{1,0:T(8,128)(2,1)} %k_hbm.1, bf16[1024,1024]{1,0:T(8,128)(2,1)} %v_hbm.1, f32[8,1,128]{2,1,0:T(1,128)} %bitcast.1, ...), custom_call_target="tpu_custom_call" | custom-call | tf_op jit(solution)/shard_map/attention/pallas_call | solution.py:318
  47.4 3.4 %write_out.1 = (bf16[1024,1024]{1,0:T(8,128)(2,1)}, bf16[1024,1024]{1,0:T(8,128)(2,1)}, bf16[1024,1024]{1,0:T(8,128)(2,1)}, bf16[1024,1024]{1,0:T(8,128)(2,1)}) custom-call(bf16[1024,1024]{1,0:T(8,128)(2,1)S(1)} %get-tuple-element.8.a, bf16[1024,1024]{1,0:T(8,128)(2,1)S(1)} %get-tuple-element.9.b, bf16[1024,1024]{1,0:T(8,128)(2,1)S(1)} %get-tuple-element.10.c, ...), custom_call_target="tpu_custom_call" | custom-call | tf_op jit(solution)/shard_map/write_out/pallas_call | solution.py:363
